TPU v7x, 128 devices: a whole 4x4x4 slice. The times are simulated.
128 devices in a mesh: frame: 32 (over x, y, z_lo), row: 4 (over z_hi, core).
Axes of the slice: x: 4, y: 4, z: 4 (z_hi: 2, z_lo: 2; z = z_hi * 2 + z_lo), core: 2. Of those that a mesh axis runs over, the one named last changes fastest.
Arguments:
- query_pre: bfloat16 [2240, 32, 16, 128], P(None, 'frame', 'row'), may hold values from -6 to 6
- key_pre: bfloat16 [2240, 32, 16, 128], P(None, 'frame', 'row'), may hold values from -80 to 80
- values: bfloat16 [2240, 32, 16, 128], P(None, 'frame', 'row'), may hold values from -1 to 2
- cotangent: bfloat16 [2240, 32, 16, 128], P(None, 'frame', 'row'), may hold values from -3072 to 3072
- kernel: bfloat16 [3, 3, 2240], replicated, may hold values from -0.29882812 to 0.59765625
Outputs:
- grad_query: bfloat16 [2240, 32, 16, 128], P(None, 'frame', 'row')
- grad_key: bfloat16 [2240, 32, 16, 128], P(None, 'frame', 'row')
- grad_values: bfloat16 [2240, 32, 16, 128], P(None, 'frame', 'row')
All inputs are finite; a program needn't handle non-finite values.
Results may differ from a plain program's by a relative error of at most 0.008.
Values may be sent and summed in bfloat16 or wider, within the bound.
A program may use at most 128 MiB of HBM per device.

v0:
```python
import jax
import jax.numpy as jnp
from jax import lax
from jax.sharding import PartitionSpec as P

HD = 32
denominator_eps = 0.001


def extended(array, sides, width):
    for axis, dim in sides:
        size, length = (lax.axis_size(axis), array.shape[dim])
        up = [(i, (i + 1) % size) for i in range(size - 1)]
        down = [(j, i) for i, j in up]
        last = lax.slice_in_dim(array, length - width, length, axis=dim)
        leading = lax.slice_in_dim(array, 0, width, axis=dim)
        before = lax.ppermute(last, axis, up)
        after = lax.ppermute(leading, axis, down)
        array = jnp.concatenate([before, array, after], axis=dim)
    return array


def conv_taps(padded, weights, flipped, row_count, col_count):
    summed = None
    for tap_row in range(3):
        for tap_col in range(3):
            start_row = 2 - tap_row if flipped else tap_row
            start_col = 2 - tap_col if flipped else tap_col
            window = padded[
                :, :, start_row : start_row + row_count, start_col : start_col + col_count
            ]
            tap_term = weights[tap_row, tap_col][:, None, None, None] * window
            summed = tap_term if summed is None else summed + tap_term
    return summed


def pad_columns(field):
    return jnp.pad(field, ((0, 0), (0, 0), (0, 0), (1, 1)))


def shards(query_pre, key_pre, values, cotangent, kernel):
    highest = lax.Precision.HIGHEST
    channels, frames, row_count, col_count = values.shape
    head_count = channels // HD
    tokens_dev = frames * row_count * col_count
    all_tokens = tokens_dev * lax.axis_size("frame") * lax.axis_size("row")
    flat = (head_count, HD, tokens_dev)
    weights = kernel.astype(jnp.float32)
    value_ext = extended(values, (("row", 2),), 1)
    value_pad = pad_columns(value_ext.astype(jnp.float32))
    mixed = conv_taps(value_pad, weights, False, row_count, col_count).reshape(flat)
    key_act = jax.nn.relu(key_pre.astype(jnp.float32)).reshape(flat)
    query_act = jax.nn.relu(query_pre.astype(jnp.float32)).reshape(flat)
    local_state = jnp.einsum("hjt,het->hje", key_act, mixed, precision=highest)
    local_sum = jnp.sum(key_act, axis=2)
    state, key_sum = lax.psum((local_state, local_sum), ("frame", "row"))
    denom = (
        jnp.einsum("hj,hjt->ht", key_sum, query_act, precision=highest)
        + denominator_eps * all_tokens
    )
    numer = jnp.einsum("hje,hjt->het", state, query_act, precision=highest)
    output = numer / denom[:, None, :]
    grad_out = cotangent.astype(jnp.float32).reshape(flat)
    grad_num = grad_out / denom[:, None, :]
    grad_den = -jnp.sum(grad_out * output, axis=1) / denom
    local_gstate = jnp.einsum("hjt,het->hje", query_act, grad_num, precision=highest)
    local_gsum = jnp.einsum("hjt,ht->hj", query_act, grad_den, precision=highest)
    grad_state, grad_sum = lax.psum((local_gstate, local_gsum), ("frame", "row"))
    grad_qact = (
        jnp.einsum("hje,het->hjt", state, grad_num, precision=highest)
        + key_sum[:, :, None] * grad_den[:, None, :]
    )
    grad_query = (
        jnp.where(query_pre.reshape(flat) > 0, grad_qact, 0.0)
        .astype(jnp.bfloat16)
        .reshape(values.shape)
    )
    grad_mixed = jnp.einsum("hje,hjt->het", grad_state, key_act, precision=highest)
    grad_kact = (
        jnp.einsum("hje,het->hjt", grad_state, mixed, precision=highest) + grad_sum[:, :, None]
    )
    grad_key = (
        jnp.where(key_pre.reshape(flat) > 0, grad_kact, 0.0)
        .astype(jnp.bfloat16)
        .reshape(values.shape)
    )
    grad_grid = grad_mixed.reshape(channels, frames, row_count, col_count)
    grad_ext = extended(grad_grid.astype(jnp.bfloat16), (("row", 2),), 1).astype(grad_grid.dtype)
    grad_values = conv_taps(pad_columns(grad_ext), weights, True, row_count, col_count).astype(
        jnp.bfloat16
    )
    return (grad_query, grad_key, grad_values)


def solution(mesh):
    return jax.shard_map(
        shards,
        mesh=mesh,
        in_specs=(
            P(None, "frame", "row", None),
            P(None, "frame", "row", None),
            P(None, "frame", "row", None),
            P(None, "frame", "row", None),
            P(),
        ),
        out_specs=(
            P(None, "frame", "row", None),
            P(None, "frame", "row", None),
            P(None, "frame", "row", None),
        ),
        check_vma=False,
    )
```

profile of v0, /device:TPU:1, one launch (start us, length us, event | category | flops | bytes accessed | tf_op | source)
XLA Modules:
  0.0 554.9 jit_solution(3331773693273662485)
XLA Ops:
  7.2 4.5 fusion.36
  16.9 5.5 collective-permute-start
  22.4 5.1 reshape.172
  27.6 18.0 %fusion.30 = (f32[2240]{0:T(1024)S(1)}, f32[2240,1,4,128]{3,2,1,0:T(4,128)}) fusion(bf16[2240,1,4,128]{3,2,1,0:T(4,128)(2,1)S(1)} %copy-done.2), kind=kLoop, calls=%fused_computation.59 | loop fusion | flops 3438400 | bytes 6890240 | tf_op jit(solution)/shard_map/reduce_sum | solution.py:55
  45.5 6.3 %reshape.164 = f32[70,32,512]{2,1,0:T(8,128)} reshape(f32[2240,1,4,128]{3,2,1,0:T(4,128)} %get-tuple-element.26) | data formatting | bytes 9175040 | tf_op jit(solution)/shard_map/reshape | solution.py:52
  52.7 4.6 convert_maximum_fusion
  57.3 6.3 %reshape.168 = f32[70,32,512]{2,1,0:T(8,128)} reshape(f32[2240,1,4,128]{3,2,1,0:T(4,128)} %convert_maximum_fusion) | data formatting | bytes 9175040 | tf_op jit(solution)/shard_map/reshape | solution.py:53
  63.7 65.3 %psum.29 = f32[70,32]{1,0:T(8,128)S(1)} all-reduce(f32[70,32]{1,0:T(8,128)S(1)} %reduce_sum.21), channel_id=1, replica_groups=mesh['frame'=32,'row'=4] {'frame','row'}, use_global_device_ids=true, to_apply=%region_2.3 | all-reduce | flops 2240 | bytes 17920 | tf_op jit(solution)/shard_map/psum | solution.py:56
  129.1 4.8 fusion.33
  134.5 8.0 %fusion.29 = f32[70,32,32]{2,1,0:T(8,128)} fusion(f32[70,32,512]{2,1,0:T(8,128)S(1)} %copy-done, f32[70,32,512]{2,1,0:T(8,128)} %reshape.172, f32[70,512]{1,0:T(8,128)S(1)} %bitcast_add_fusion), kind=kOutput, calls=%fused_computation.56 | convolution fusion | flops 441548800 | bytes 9605120 | tf_op jit(solution)/shard_map/hjt,het->hje/dot_general | solution.py:66
  144.1 5.7 %copy.25 = bf16[2240,1,1,128]{3,2,1,0:T(2,128)(2,1)S(1)} copy(bf16[2240,1,1,128]{3,0,2,1:T(8,128)(2,1)} %collective-permute-done.1) | data formatting | bytes 1146880 | tf_op jit(solution)/shard_map/ppermute | solution.py:18
  149.8 5.9 %copy.24 = bf16[2240,1,1,128]{3,2,1,0:T(2,128)(2,1)S(1)} copy(bf16[2240,1,1,128]{3,0,2,1:T(8,128)(2,1)} %collective-permute-done) | data formatting | bytes 1146880 | tf_op jit(solution)/shard_map/ppermute | solution.py:17
  155.8 3.6 maximum_convert_fusion
  159.5 41.7 %fusion.8 = f32[2240,1,4,128]{3,2,1,0:T(4,128)} fusion(f32[2240,1,6,128]{3,2,1,0:T(8,128)S(1)} %maximum_convert_fusion, f32[2240]{0:T(1024)S(1)} %get-tuple-element.13, f32[2240]{0:T(1024)S(1)} %get-tuple-element.14, f32[2240]{0:T(1024)S(1)} %get-tuple-element.15, f32[2240]{0:T(1024)S(1)} %get-tuple-element.16, f32[2240]{0:T(1024)S(1)} %get-tuple-element.17, ...), kind=kLoop, calls=%fused_computation.20 | loop fusion | flops 19496960 | bytes 27635712 | tf_op jit(solution)/shard_map/add | solution.py:33
  201.2 6.3 %reshape.165 = f32[70,32,512]{2,1,0:T(8,128)} reshape(f32[2240,1,4,128]{3,2,1,0:T(4,128)} %fusion.8) | data formatting | bytes 9175040 | tf_op jit(solution)/shard_map/reshape | solution.py:51
  207.5 9.0 %fusion.37 = f32[70,32,32]{2,1,0:T(8,128)} fusion(f32[70,32,512]{2,1,0:T(8,128)} %reshape.164, f32[70,32,512]{2,1,0:T(8,128)} %reshape.165), kind=kOutput, calls=%fused_computation.78 | convolution fusion | flops 440401920 | bytes 9461760 | tf_op jit(solution)/shard_map/hjt,het->hje/dot_general | solution.py:54
  222.3 4.8 gt.15
  227.1 138.8 %all-reduce.5.cloned.1.call-done = (f32[70,32,32]{2,1,0:T(8,128)}, f32[70,32,32]{2,1,0:T(8,128)}) async-done(((f32[70,32,32]{2,1,0:T(8,128)}, f32[70,32,32]{2,1,0:T(8,128)}), (f32[70,32,32]{2,1,0:T(8,128)}, f32[70,32,32]{2,1,0:T(8,128)})) %all-reduce.5.cloned.1.call-update) | async-done | bytes 573456 | tf_op jit(solution)/shard_map/psum | solution.py:56
  365.9 8.2 %multiply_reduce_fusion = f32[70,512]{1,0:T(8,128)S(1)} fusion(f32[70,32,512]{2,1,0:T(8,128)} %reshape.172, f32[70,32,32]{2,1,0:T(8,128)} %get-tuple-element.21, f32[70,32,512]{2,1,0:T(8,128)} %reshape.168, f32[70,512]{1,0:T(8,128)S(1)} %copy-done.10), kind=kOutput, calls=%fused_computation.50 | convolution fusion | flops 443806720 | bytes 9748480 | tf_op jit(solution)/shard_map/hje,hjt->het/dot_general | solution.py:61
  374.9 5.2 convolution_convert_fusion
  380.0 4.1 convert_element_type.73
  390.6 4.4 collective-permute-start.2
  395.1 8.6 %select_convert_fusion.1 = bf16[70,32,512]{2,1,0:T(8,128)(2,1)} fusion(pred[70,32,512]{2,1,0:T(32,128)(4,1)S(1)} %copy-done.7, f32[70,512]{1,0:T(8,128)S(1)} %copy-done.8, f32[70,32]{1,0:T(8,128)S(1)} %psum.29, f32[70,32,32]{2,1,0:T(8,128)S(1)} %copy-done.25, f32[70,32,512]{2,1,0:T(8,128)} %reshape.172, f32[70,512]{1,0:T(8,128)S(1)} %copy-done.11), kind=kOutput, calls=%fused_computation.49 | convolution fusion | flops 446136320 | bytes 8610560 | tf_op jit(solution)/shard_map/hje,het->hjt/dot_general | solution.py:70
  403.7 4.1 fusion.31
  407.7 5.1 reshape.169
  412.9 64.3 %psum.31 = f32[70,32]{1,0:T(8,128)S(1)} all-reduce(f32[70,32]{1,0:T(8,128)S(1)} %bitcast.32), channel_id=1, replica_groups=mesh['frame'=32,'row'=4] {'frame','row'}, use_global_device_ids=true, to_apply=%region_5.6 | all-reduce | flops 2240 | bytes 17920 | tf_op jit(solution)/shard_map/psum | solution.py:68
  477.2 8.6 %select_convert_fusion = bf16[70,32,512]{2,1,0:T(8,128)(2,1)} fusion(pred[70,32,512]{2,1,0:T(32,128)(4,1)S(1)} %gt.15, f32[70,32]{1,0:T(8,128)S(1)} %psum.31, f32[70,32,32]{2,1,0:T(8,128)} %get-tuple-element.22, f32[70,32,512]{2,1,0:T(8,128)} %reshape.165), kind=kOutput, calls=%fused_computation.48 | convolution fusion | flops 443842560 | bytes 8323840 | tf_op jit(solution)/shard_map/hje,het->hjt/dot_general | solution.py:80
  485.8 5.1 reshape.170
  490.9 5.7 %copy.32 = bf16[2240,1,1,128]{3,2,1,0:T(2,128)(2,1)S(1)} copy(bf16[2240,1,1,128]{3,0,2,1:T(8,128)(2,1)} %collective-permute-done.3) | data formatting | bytes 1146880 | tf_op jit(solution)/shard_map/ppermute | solution.py:18
  496.7 5.7 %copy.30 = bf16[2240,1,1,128]{3,2,1,0:T(2,128)(2,1)S(1)} copy(bf16[2240,1,1,128]{3,0,2,1:T(8,128)(2,1)} %collective-permute-done.2) | data formatting | bytes 1146880 | tf_op jit(solution)/shard_map/ppermute | solution.py:17
  502.5 3.6 maximum_convert_fusion.1
  506.2 41.7 %fusion.28 = bf16[2240,1,4,128]{3,2,1,0:T(4,128)(2,1)} fusion(f32[2240,1,6,128]{3,2,1,0:T(8,128)S(1)} %maximum_convert_fusion.1, f32[2240]{0:T(1024)S(1)} %get-tuple-element.13, f32[2240]{0:T(1024)S(1)} %get-tuple-element.14, f32[2240]{0:T(1024)S(1)} %copy-done.13, f32[2240]{0:T(1024)S(1)} %copy-done.15, f32[2240]{0:T(1024)S(1)} %copy-done.17, ...), kind=kLoop, calls=%fused_computation.53 | loop fusion | flops 20643840 | bytes 25341952 | tf_op jit(solution)/shard_map/convert_element_type | solution.py:89
  (84 shorter events, 21.3 us)
Async XLA Ops:
  7.2 358.7 %all-reduce.5.cloned.1.call-start = ((), (), s32[]{:S(2)}) async-start(), calls=%async_computation | async-start | bytes 4587520 | tf_op jit(solution)/shard_map/psum | solution.py:56
  12.6 14.9 %copy-start.2 = (bf16[2240,1,4,128]{3,2,1,0:T(4,128)(2,1)S(1)}, bf16[2240,1,4,128]{3,2,1,0:T(4,128)(2,1)}, u32[]{:S(2)}) copy-start(bf16[2240,1,4,128]{3,2,1,0:T(4,128)(2,1)} %param.6) | copy-start | bytes 6881284
  12.6 131.5 %collective-permute-start.1 = (bf16[2240,1,1,128]{3,0,2,1:T(8,128)(2,1)}, bf16[2240,1,1,128]{3,0,2,1:T(8,128)(2,1)}, u32[]{:S(2)}, u32[]{:S(2)}) collective-permute-start(bf16[2240,1,1,128]{3,0,2,1:T(8,128)(2,1)} %copy.42), channel_id=1, source_target_pairs={{1,0},{2,1},{3,2},{5,4},{6,5},{7,6},{9,8},{10,9},{11,10},{13,12},{... | collective-permute-start | bytes 1720328 | tf_op jit(solution)/shard_map/ppermute | solution.py:18
  16.9 132.9 %collective-permute-start = (bf16[2240,1,1,128]{3,0,2,1:T(8,128)(2,1)}, bf16[2240,1,1,128]{3,0,2,1:T(8,128)(2,1)}, u32[]{:S(2)}, u32[]{:S(2)}) collective-permute-start(bf16[2240,1,1,128]{3,0,2,1:T(8,128)(2,1)} %copy.41), channel_id=1, source_target_pairs={{0,1},{1,2},{2,3},{4,5},{5,6},{6,7},{8,9},{9,10},{10,11},{12,13},{... | collective-permute-start | bytes 1720328 | tf_op jit(solution)/shard_map/ppermute | solution.py:17
  45.5 6.3 %copy-start.24 = (bf16[3,3,2240]{2,1,0:T(4,128)(2,1)S(1)}, bf16[3,3,2240]{2,1,0:T(4,128)(2,1)}, u32[]{:S(2)}) copy-start(bf16[3,3,2240]{2,1,0:T(4,128)(2,1)} %param.9) | copy-start | bytes 120964
  52.7 106.8 %copy-start.12 = (f32[2240]{0:T(1024)}, f32[2240]{0:T(1024)S(1)}, u32[]{:S(2)}) copy-start(f32[2240]{0:T(1024)S(1)} %get-tuple-element.15) | copy-start | bytes 26884
  52.7 106.8 %copy-start.14 = (f32[2240]{0:T(1024)}, f32[2240]{0:T(1024)S(1)}, u32[]{:S(2)}) copy-start(f32[2240]{0:T(1024)S(1)} %get-tuple-element.16) | copy-start | bytes 26884
  52.7 106.8 %copy-start.16 = (f32[2240]{0:T(1024)}, f32[2240]{0:T(1024)S(1)}, u32[]{:S(2)}) copy-start(f32[2240]{0:T(1024)S(1)} %get-tuple-element.17) | copy-start | bytes 26884
  129.1 5.5 copy-start
  134.5 8.0 %copy-start.9 = (f32[70,512]{1,0:T(8,128)}, f32[70,512]{1,0:T(8,128)S(1)}, u32[]{:S(2)}) copy-start(f32[70,512]{1,0:T(8,128)S(1)} %bitcast_add_fusion) | copy-start | bytes 430084
  134.5 8.0 %copy-start.3 = (bf16[2240,1,4,128]{3,2,1,0:T(4,128)(2,1)S(1)}, bf16[2240,1,4,128]{3,2,1,0:T(4,128)(2,1)}, u32[]{:S(2)}) copy-start(bf16[2240,1,4,128]{3,2,1,0:T(4,128)(2,1)} %param.5) | copy-start | bytes 6881284
  142.5 13.2 %copy-start.1 = (bf16[2240,1,4,128]{3,2,1,0:T(4,128)(2,1)S(1)}, bf16[2240,1,4,128]{3,2,1,0:T(4,128)(2,1)}, u32[]{:S(2)}) copy-start(bf16[2240,1,4,128]{3,2,1,0:T(4,128)(2,1)} %param.7) | copy-start | bytes 6881284
  155.8 3.7 copy-start.18
  155.8 3.7 copy-start.20
  155.8 3.7 copy-start.22
  219.0 146.9 %copy-start.10 = (f32[70,512]{1,0:T(8,128)S(1)}, f32[70,512]{1,0:T(8,128)}, u32[]{:S(2)}) copy-start(f32[70,512]{1,0:T(8,128)} %copy-done.9) | copy-start | bytes 430084
  222.3 152.6 %slice-start.2 = ((s8[4587520]{0:T(1024)(128)(4,1)}), s8[393216]{0:T(1024)(128)(4,1)S(1)}, s32[]{:S(2)}) async-start(s8[4587520]{0:T(1024)(128)(4,1)} %bitcast.26), calls=%async_computation.3 | async-start | bytes 786432
  365.9 8.2 %copy-start.6 = (f32[70,1,512]{2,1,0:T(1,128)S(1)}, f32[70,1,512]{2,1,0:T(1,128)}, u32[]{:S(2)}) copy-start(f32[70,1,512]{2,1,0:T(1,128)} %copy-done.5) | copy-start | bytes 430084
  365.9 8.9 %slice-start.3 = ((s8[4587520]{0:T(1024)(128)(4,1)}), s8[4194304]{0:T(1024)(128)(4,1)S(1)}, s32[]{:S(2)}) async-start(s8[4587520]{0:T(1024)(128)(4,1)} %bitcast.26), calls=%async_computation.4 | async-start | bytes 8388608
  365.9 8.9 %copy-start.4 = (f32[70,32,32]{2,1,0:T(8,128)S(1)}, f32[70,32,32]{2,1,0:T(8,128)}, u32[]{:S(2)}) copy-start(f32[70,32,32]{2,1,0:T(8,128)} %get-tuple-element.22) | copy-start | bytes 860164
  384.2 10.9 %copy-start.7 = (pred[70,32,512]{2,1,0:T(32,128)(4,1)S(1)}, pred[70,32,512]{2,1,0:T(32,128)(4,1)}, u32[]{:S(2)}) copy-start(pred[70,32,512]{2,1,0:T(32,128)(4,1)} %gt.13) | copy-start | bytes 3440644
  384.2 10.9 %copy-start.8 = (f32[70,512]{1,0:T(8,128)S(1)}, f32[70,512]{1,0:T(8,128)}, u32[]{:S(2)}) copy-start(f32[70,512]{1,0:T(8,128)} %negate_divide_fusion) | copy-start | bytes 430084
  384.2 10.9 %copy-start.11 = (f32[70,512]{1,0:T(8,128)S(1)}, f32[70,512]{1,0:T(8,128)}, u32[]{:S(2)}) copy-start(f32[70,512]{1,0:T(8,128)} %copy-done.9) | copy-start | bytes 430084
  384.2 10.9 %copy-start.25 = (f32[70,32,32]{2,1,0:T(8,128)S(1)}, f32[70,32,32]{2,1,0:T(8,128)}, u32[]{:S(2)}) copy-start(f32[70,32,32]{2,1,0:T(8,128)} %get-tuple-element.21) | copy-start | bytes 860164
  386.8 104.2 %collective-permute-start.3 = (bf16[2240,1,1,128]{3,0,2,1:T(8,128)(2,1)}, bf16[2240,1,1,128]{3,0,2,1:T(8,128)(2,1)}, u32[]{:S(2)}, u32[]{:S(2)}) collective-permute-start(bf16[2240,1,1,128]{3,0,2,1:T(8,128)(2,1)} %copy.44), channel_id=1, source_target_pairs={{1,0},{2,1},{3,2},{5,4},{6,5},{7,6},{9,8},{10,9},{11,10},{13,12},{... | collective-permute-start | bytes 1720328 | tf_op jit(solution)/shard_map/ppermute | solution.py:18
  389.7 13.9 %slice-start = ((s8[4587520]{0:T(1024)(128)(4,1)}), s8[4194304]{0:T(1024)(128)(4,1)S(1)}, s32[]{:S(2)}) async-start(s8[4587520]{0:T(1024)(128)(4,1)} %bitcast.24), calls=%async_computation.1 | async-start | bytes 8388608
  390.6 13.0 %slice-start.1 = ((s8[4587520]{0:T(1024)(128)(4,1)}), s8[393216]{0:T(1024)(128)(4,1)S(1)}, s32[]{:S(2)}) async-start(s8[4587520]{0:T(1024)(128)(4,1)} %bitcast.24), calls=%async_computation.2 | async-start | bytes 786432
  390.6 106.1 %collective-permute-start.2 = (bf16[2240,1,1,128]{3,0,2,1:T(8,128)(2,1)}, bf16[2240,1,1,128]{3,0,2,1:T(8,128)(2,1)}, u32[]{:S(2)}, u32[]{:S(2)}) collective-permute-start(bf16[2240,1,1,128]{3,0,2,1:T(8,128)(2,1)} %copy.43), channel_id=1, source_target_pairs={{0,1},{1,2},{2,3},{4,5},{5,6},{6,7},{8,9},{9,10},{10,11},{12,13},{... | collective-permute-start | bytes 1720328 | tf_op jit(solution)/shard_map/ppermute | solution.py:17
  502.4 3.7 copy-start.13
  502.4 3.7 copy-start.15
  502.4 3.7 copy-start.17
  502.4 3.7 copy-start.19
  (3 other events, 8.0 us)
Sparse Core Ops, SparseCore 0:
  216.6 149.2 all-reduce.4
where the time goes:
time: 562 us; the launch traced here: 555 us
  waiting for transfers between devices  139 us (25%)
  blocking collectives  130 us (23%)
  other arithmetic  118 us (21%)
  local copies, waits for them, and re-layouts  81 us (14%)
  matrix products  56.3 us (10%)
  starting transfers between devices  16.3 us (3%)
  between operations  14.7 us (3%)
    psum x1, waiting for transfers between devices, shards(): state, key_sum = lax.psum((local_state, local_sum), ('frame', 'row'))  139 us
    psum x1, blocking collectives, shards(): state, key_sum = lax.psum((local_state, local_sum), ('frame', 'row'))  65.3 us
    psum x1, blocking collectives, shards(): lax.psum((local_gstate, local_gsum), ('frame', 'row'))  64.3 us
    convert_element_type x1, other arithmetic, shards(): conv_taps(pad_columns(grad_ext), weights, True, row_count, col_count)  41.7 us
    add x1, other arithmetic, conv_taps(): summed = tap_term if summed is None else summed + tap_term  41.7 us
    reduce_sum x1, other arithmetic, shards(): local_sum = jnp.sum(key_act, axis=2)  18 us
    ppermute x2, local copies, waits for them, and re-layouts, extended(): before = lax.ppermute(last, axis, up)  11.7 us
    ppermute x2, local copies, waits for them, and re-layouts, extended(): after = lax.ppermute(leading, axis, down)  11.4 us
  transfers between devices with their start and end apart: 5, of which 1 were waited for; matrix products, arithmetic and copies ran while one was open for 20% of the time, Pallas kernels for 0%

commit v1 on v0

--- a/solution.py
+++ b/solution.py
@@ -65,7 +65,7 @@
     grad_den = -jnp.sum(grad_out * output, axis=1) / denom
     local_gstate = jnp.einsum("hjt,het->hje", query_act, grad_num, precision=highest)
     local_gsum = jnp.einsum("hjt,ht->hj", query_act, grad_den, precision=highest)
-    grad_state, grad_sum = lax.psum((local_gstate, local_gsum), ("frame", "row"))
+    grad_state, grad_sum = lax.psum(lax.psum((local_gstate, local_gsum), "frame"), "row")
     grad_qact = (
         jnp.einsum("hje,het->hjt", state, grad_num, precision=highest)
         + key_sum[:, :, None] * grad_den[:, None, :]

time: 562 us -> 973 us (1.73)
  waiting for transfers between devices: 139 us -> 450 us
  blocking collectives: 130 us -> 238 us
  other arithmetic: 118 us -> 97.2 us
  starting transfers between devices: 16.3 us -> 34.1 us
    psum x0 -> x2, waiting for transfers between devices: none -> 312 us  [the longest x1 279 us: shards(): lax.psum((local_gstate, local_gsum), 'frame')]
    psum x1 -> x2, blocking collectives: 64.3 us -> 169 us  [the longest x1 128 us: shards(): lax.psum((local_gstate, local_gsum), 'frame')]
    add x1 -> x0, other arithmetic: 41.7 us -> none  [conv_taps(): summed = tap_term if summed is None else summed + tap_term]
    ppermute x2, starting transfers between devices: 9.93 us -> 29.9 us  [extended(): before = lax.ppermute(last, axis, up)]
    convert_element_type x1, other arithmetic: 41.7 us -> 61.2 us  [shards(): conv_taps(pad_columns(grad_ext), weights, True, row_count, col_count)]
  transfers between devices with their start and end apart: 5 -> 7, of which waited for: 1 -> 3; matrix products, arithmetic and copies ran while one was open for 20% -> 6% of each run, Pallas kernels for 0% -> 0%
where the time goes in v1:
time: 973 us; the launch traced here: 968 us
  waiting for transfers between devices  450 us (46%)
  blocking collectives  238 us (24%)
  other arithmetic  97.2 us (10%)
  local copies, waits for them, and re-layouts  75.7 us (8%)
  matrix products  58.4 us (6%)
  starting transfers between devices  34.1 us (4%)
  between operations  14.3 us (1%)
    psum x1, waiting for transfers between devices, shards(): lax.psum((local_gstate, local_gsum), 'frame')  279 us
    psum x1, waiting for transfers between devices, shards(): state, key_sum = lax.psum((local_state, local_sum), ('frame', 'row'))  138 us
    psum x1, blocking collectives, shards(): lax.psum((local_gstate, local_gsum), 'frame')  128 us
    psum x1, blocking collectives, shards(): state, key_sum = lax.psum((local_state, local_sum), ('frame', 'row'))  69.2 us
    convert_element_type x1, other arithmetic, shards(): conv_taps(pad_columns(grad_ext), weights, True, row_count, col_count)  61.2 us
    psum x1, blocking collectives, shards(): lax.psum(lax.psum((local_gstate, local_gsum), 'frame'), 'row')  40.9 us
    psum x1, waiting for transfers between devices, shards(): lax.psum(lax.psum((local_gstate, local_gsum), 'frame'), 'row')  32.6 us
    ppermute x2, starting transfers between devices, extended(): before = lax.ppermute(last, axis, up)  29.9 us
  transfers between devices with their start and end apart: 7, of which 3 were waited for; matrix products, arithmetic and copies ran while one was open for 6% of the time, Pallas kernels for 0%

profile of v1, /device:TPU:1, one launch (start us, length us, event | category | flops | bytes accessed | tf_op | source)
XLA Modules:
  0.0 968.0 jit_solution(16737044574475533383)
XLA Ops:
  7.2 4.6 convert_maximum_fusion
  11.8 6.5 reshape.168
  18.3 17.9 %fusion.30 = (f32[2240]{0:T(1024)S(1)}, f32[2240,1,4,128]{3,2,1,0:T(4,128)}) fusion(bf16[2240,1,4,128]{3,2,1,0:T(4,128)(2,1)S(1)} %copy-done), kind=kLoop, calls=%fused_computation.59 | loop fusion | flops 3438400 | bytes 6890240 | tf_op jit(solution)/shard_map/reduce_sum | solution.py:55
  36.2 69.2 %psum.43 = f32[70,32]{1,0:T(8,128)S(1)} all-reduce(f32[70,32]{1,0:T(8,128)S(1)} %reduce_sum.21), channel_id=1, replica_groups=mesh['frame'=32,'row'=4] {'frame','row'}, use_global_device_ids=true, to_apply=%region_2.3 | all-reduce | flops 2240 | bytes 17920 | tf_op jit(solution)/shard_map/psum | solution.py:56
  105.4 4.6 fusion.33
  110.7 2.8 reshape.172
  113.5 9.3 fusion.29
  122.9 279.4 %all-reduce.8.cloned.1.call-done = f32[70,32,32]{2,1,0:T(8,128)} async-done(((f32[70,32,32]{2,1,0:T(8,128)}), f32[70,32,32]{2,1,0:T(8,128)}) %all-reduce.8.cloned.1.call-update) | async-done | bytes 286736 | tf_op jit(solution)/shard_map/psum | solution.py:68
  404.9 26.5 %collective-permute-start = (bf16[2240,1,1,128]{3,0,2,1:T(8,128)(2,1)}, bf16[2240,1,1,128]{3,0,2,1:T(8,128)(2,1)}, u32[]{:S(2)}, u32[]{:S(2)}) collective-permute-start(bf16[2240,1,1,128]{3,0,2,1:T(8,128)(2,1)} %copy.41), channel_id=1, source_target_pairs={{0,1},{1,2},{2,3},{4,5},{5,6},{6,7},{8,9},{9,10},{10,11},{12,13},{... | collective-permute-start | bytes 1720328 | tf_op jit(solution)/shard_map/ppermute | solution.py:17
  434.5 6.3 reshape.164
  440.8 32.6 %all-reduce.10.cloned.1.call-done = f32[70,32,32]{2,1,0:T(8,128)} async-done(((f32[70,32,32]{2,1,0:T(8,128)}), f32[70,32,32]{2,1,0:T(8,128)}) %all-reduce.10.cloned.1.call-update) | async-done | bytes 286736 | tf_op jit(solution)/shard_map/psum | solution.py:68
  473.4 7.2 convolution_convert_fusion
  480.6 4.1 convert_element_type.73
  486.5 3.4 collective-permute-start.2
  493.8 5.7 copy.24
  499.5 5.7 copy.25
  505.2 3.6 maximum_convert_fusion
  508.9 9.3 copy.30
  518.2 9.3 copy.32
  527.5 5.7 maximum_convert_fusion.1
  533.2 61.2 %fusion.28 = (bf16[2240,1,4,128]{3,2,1,0:T(4,128)(2,1)}, f32[2240,1,4,128]{3,2,1,0:T(4,128)}) fusion(f32[2240,1,6,128]{3,2,1,0:T(8,128)} %maximum_convert_fusion.1, f32[2240]{0:T(1024)S(1)} %get-tuple-element.13, f32[2240]{0:T(1024)S(1)} %get-tuple-element.14, f32[2240]{0:T(1024)S(1)} %get-tuple-element.15, f32[2240]{0:T(1024)S(1)} %get-tuple-element.16, ...), kind=kLoop, calls=%fused_computation.53 | loop fusion | flops 40140800 | bytes 52867072 | tf_op jit(solution)/shard_map/convert_element_type | solution.py:89
  594.4 6.7 reshape.165
  601.2 9.1 fusion.37
  612.8 3.3 gt.15
  616.1 5.6 gt.13
  621.7 138.3 %all-reduce.6.cloned.1.call-done = f32[70,32,32]{2,1,0:T(8,128)} async-done(((f32[70,32,32]{2,1,0:T(8,128)}), f32[70,32,32]{2,1,0:T(8,128)}) %all-reduce.6.cloned.1.call-update) | async-done | bytes 286736 | tf_op jit(solution)/shard_map/psum | solution.py:56
  760.0 7.6 multiply_reduce_fusion
  767.7 5.9 fusion.31
  773.6 127.9 %psum.46 = f32[70,32]{1,0:T(8,128)S(1)} all-reduce(f32[70,32]{1,0:T(8,128)S(1)} %bitcast.28), channel_id=1, replica_groups=mesh['frame'=32,'row'=4] {'frame'}, use_global_device_ids=true, to_apply=%region_6.7 | all-reduce | flops 2240 | bytes 17920 | tf_op jit(solution)/shard_map/psum | solution.py:68
  901.5 40.9 %psum.47 = f32[70,32]{1,0:T(8,128)S(1)} all-reduce(f32[70,32]{1,0:T(8,128)S(1)} %psum.46), channel_id=1, replica_groups=mesh['frame'=32,'row'=4] {'row'}, use_global_device_ids=true, to_apply=%region_7.8 | all-reduce | flops 2240 | bytes 17920 | tf_op jit(solution)/shard_map/psum | solution.py:68
  942.4 7.2 select_convert_fusion
  951.7 7.5 select_convert_fusion.1
  (56 shorter events, 18.8 us)
Async XLA Ops:
  7.2 395.1 %all-reduce.8.cloned.1.call-start = ((), (), s32[]{:S(2)}) async-start(), calls=%async_computation.1 | async-start | bytes 2293760 | tf_op jit(solution)/shard_map/psum | solution.py:68
  11.8 6.5 copy-start
  36.2 74.5 %copy-start.6 = (bf16[2240,1,4,128]{3,2,1,0:T(4,128)(2,1)S(1)}, bf16[2240,1,4,128]{3,2,1,0:T(4,128)(2,1)}, u32[]{:S(2)}) copy-start(bf16[2240,1,4,128]{3,2,1,0:T(4,128)(2,1)} %param.8) | copy-start | bytes 6881284
  110.0 0.6 copy-start.7
  110.7 12.1 %copy-start.11 = (f32[70,512]{1,0:T(8,128)}, f32[70,512]{1,0:T(8,128)S(1)}, u32[]{:S(2)}) copy-start(f32[70,512]{1,0:T(8,128)S(1)} %bitcast_add_fusion) | copy-start | bytes 430084
  113.5 288.8 %copy-start.2 = (bf16[2240,1,4,128]{3,2,1,0:T(4,128)(2,1)S(1)}, bf16[2240,1,4,128]{3,2,1,0:T(4,128)(2,1)}, u32[]{:S(2)}) copy-start(bf16[2240,1,4,128]{3,2,1,0:T(4,128)(2,1)} %param.7) | copy-start | bytes 6881284
  122.9 350.6 %all-reduce.10.cloned.1.call-start = ((), (), s32[]{:S(2)}) async-start(), calls=%async_computation.2 | async-start | bytes 2293760 | tf_op jit(solution)/shard_map/psum | solution.py:68
  402.3 357.7 %all-reduce.6.cloned.1.call-start = ((), (), s32[]{:S(2)}) async-start(), calls=%async_computation | async-start | bytes 2293760 | tf_op jit(solution)/shard_map/psum | solution.py:56
  404.9 88.8 %collective-permute-start = (bf16[2240,1,1,128]{3,0,2,1:T(8,128)(2,1)}, bf16[2240,1,1,128]{3,0,2,1:T(8,128)(2,1)}, u32[]{:S(2)}, u32[]{:S(2)}) collective-permute-start(bf16[2240,1,1,128]{3,0,2,1:T(8,128)(2,1)} %copy.41), channel_id=1, source_target_pairs={{0,1},{1,2},{2,3},{4,5},{5,6},{6,7},{8,9},{9,10},{10,11},{12,13},{... | collective-permute-start | bytes 1720328 | tf_op jit(solution)/shard_map/ppermute | solution.py:17
  432.4 67.1 %collective-permute-start.1 = (bf16[2240,1,1,128]{3,0,2,1:T(8,128)(2,1)}, bf16[2240,1,1,128]{3,0,2,1:T(8,128)(2,1)}, u32[]{:S(2)}, u32[]{:S(2)}) collective-permute-start(bf16[2240,1,1,128]{3,0,2,1:T(8,128)(2,1)} %copy.42), channel_id=1, source_target_pairs={{1,0},{2,1},{3,2},{5,4},{6,5},{7,6},{9,8},{10,9},{11,10},{13,12},{... | collective-permute-start | bytes 1720328 | tf_op jit(solution)/shard_map/ppermute | solution.py:18
  484.7 7.2 copy-start.1
  486.4 7.1 copy-start.13
  486.5 18.7 %copy-start.3 = (bf16[2240,1,4,128]{3,2,1,0:T(4,128)(2,1)S(1)}, bf16[2240,1,4,128]{3,2,1,0:T(4,128)(2,1)}, u32[]{:S(2)}) copy-start(bf16[2240,1,4,128]{3,2,1,0:T(4,128)(2,1)} %param.7) | copy-start | bytes 6881284
  486.5 22.3 %collective-permute-start.2 = (bf16[2240,1,1,128]{3,0,2,1:T(8,128)(2,1)S(1)}, bf16[2240,1,1,128]{3,0,2,1:T(8,128)(2,1)S(1)}, u32[]{:S(2)}, u32[]{:S(2)}) collective-permute-start(bf16[2240,1,1,128]{3,0,2,1:T(8,128)(2,1)S(1)} %copy.43), channel_id=1, source_target_pairs={{0,1},{1,2},{2,3},{4,5},{5,6},{6,7},{8,9},{9,10},{10,11},{12,13},{... | collective-permute-start | bytes 1720328 | tf_op jit(solution)/shard_map/ppermute | solution.py:17
  490.0 28.2 %collective-permute-start.3 = (bf16[2240,1,1,128]{3,0,2,1:T(8,128)(2,1)S(1)}, bf16[2240,1,1,128]{3,0,2,1:T(8,128)(2,1)S(1)}, u32[]{:S(2)}, u32[]{:S(2)}) collective-permute-start(bf16[2240,1,1,128]{3,0,2,1:T(8,128)(2,1)S(1)} %copy.44), channel_id=1, source_target_pairs={{1,0},{2,1},{3,2},{5,4},{6,5},{7,6},{9,8},{10,9},{11,10},{13,12},{... | collective-permute-start | bytes 1720328 | tf_op jit(solution)/shard_map/ppermute | solution.py:18
  601.1 9.1 copy-start.4
  612.8 147.2 %copy-start.12 = (f32[70,512]{1,0:T(8,128)S(1)}, f32[70,512]{1,0:T(8,128)}, u32[]{:S(2)}) copy-start(f32[70,512]{1,0:T(8,128)} %copy-done.11) | copy-start | bytes 430084
  621.7 145.9 %copy-start.8 = (f32[70,1,512]{2,1,0:T(1,128)S(1)}, f32[70,1,512]{2,1,0:T(1,128)}, u32[]{:S(2)}) copy-start(f32[70,1,512]{2,1,0:T(1,128)} %copy-done.7) | copy-start | bytes 430084
  767.6 174.8 %copy-start.5 = (pred[70,32,512]{2,1,0:T(32,128)(4,1)S(1)}, pred[70,32,512]{2,1,0:T(32,128)(4,1)}, u32[]{:S(2)}) copy-start(pred[70,32,512]{2,1,0:T(32,128)(4,1)} %gt.15) | copy-start | bytes 3440644
  767.7 133.8 %copy-start.10 = (f32[70,512]{1,0:T(8,128)}, f32[70,512]{1,0:T(8,128)S(1)}, u32[]{:S(2)}) copy-start(f32[70,512]{1,0:T(8,128)S(1)} %negate_divide_fusion) | copy-start | bytes 430084
  949.6 2.1 copy-start.9
Sparse Core Ops, SparseCore 0:
  123.0 279.2 all-reduce.7
  404.8 68.5 all-reduce.9
  610.4 149.5 all-reduce.5
